TPU v7x, 512 devices: a whole 4x4x16 slice. The times are simulated.
512 devices in a mesh: tr: 64 (over x, z), ct: 8 (over y, core).
Axes of the slice: x: 4, y: 4, z: 16, core: 2. Of those that a mesh axis runs over, the one named last changes fastest.
Arguments:
- amplitudes: bfloat16 [8, 4096, 2, 4096], P(None, 'tr', None, 'ct'), may hold values from -6 to 6
- cycle_integrals: bfloat16 [2, 4096, 1, 4096], P(None, 'ct', None, 'tr'), may hold values from -0.0625 to 0.0625
- pair_live: int32 [8, 64], replicated, may hold values 0 or 1
Outputs:
- permuted: bfloat16 [8, 4096, 1, 4096], P('ct', 'tr')
All inputs are finite; a program needn't handle non-finite values.
Results may differ from a plain program's by a relative error of at most 0.017.
Values may be sent and summed in bfloat16 or wider, within the bound.
A program may use at most 64 MiB of HBM per device.

v0:
```python
import jax
import jax.numpy as jnp
from jax import lax
from jax.sharding import PartitionSpec as P


def per_device(amplitudes, cycle_integrals, pair_live):
    tile_size = amplitudes.shape[1]
    block_cols = amplitudes.shape[3]
    occ_k = amplitudes.shape[2]
    row_index = lax.axis_index("tr")
    col_index = lax.axis_index("ct")
    row_live = lax.dynamic_slice_in_dim(pair_live, row_index, 1, 1).astype(jnp.bfloat16)
    col_full = jnp.repeat(pair_live[:occ_k], tile_size, axis=1)
    col_live = lax.dynamic_slice_in_dim(col_full, col_index * block_cols, block_cols, 1).astype(
        jnp.bfloat16
    )
    masked = amplitudes * row_live[:, :, None, None] * col_live[None, None, :, :]
    partial_value = jnp.einsum(
        "iakc,kcjb->iajb",
        masked,
        lax.all_gather(cycle_integrals, "tr", axis=3, tiled=True),
        preferred_element_type=jnp.float32,
    )
    moved_parts = lax.all_to_all(
        partial_value.astype(jnp.bfloat16), "tr", split_axis=3, concat_axis=1, tiled=True
    )
    moved = lax.psum_scatter(
        moved_parts.astype(jnp.float32).astype(jnp.bfloat16), "ct", scatter_dimension=0, tiled=True
    )
    return jnp.transpose(moved, (0, 3, 2, 1))


def solution(mesh):
    return jax.shard_map(
        per_device,
        mesh=mesh,
        in_specs=(P(None, "tr", None, "ct"), P(None, "ct", None, "tr"), P()),
        out_specs=P("ct", "tr", None, None),
        check_vma=False,
    )
```

profile of v0, /device:TPU:2, one launch (start us, length us, event | category | flops | bytes accessed | tf_op | source)
XLA Modules:
  0.0 500.7 jit_solution(14204285625697679978)
XLA Ops:
  6.5 0.0 all-gather.2.cloned.1.call-start
  6.5 1.7 copy.7
  8.2 0.0 all-gather.2.cloned.1.call-update
  8.3 0.0 reduce-scatter.2.cloned.1.call-start
  8.3 0.7 slice.3
  9.0 0.9 fusion.8
  9.9 0.1 broadcast_in_dim.2
  9.9 0.1 reshape.10
  10.1 2.3 multiply_multiply_fusion
  12.4 158.5 %all-gather.2.cloned.1.call-done = bf16[2,512,1,4096]{1,0,2,3:T(2,128)(2,1)} async-done(((bf16[2,512,1,64]{1,0,2,3:T(2,128)(2,1)}), bf16[2,512,1,4096]{1,0,2,3:T(2,128)(2,1)}) %all-gather.2.cloned.1.call-update) | async-done | bytes 8388624 | tf_op jit(solution)/shard_map/all_gather | solution.py:22
  170.8 21.3 %copy.8 = bf16[2,512,1,4096]{3,1,0,2:T(8,128)(2,1)} copy(bf16[2,512,1,4096]{1,0,2,3:T(2,128)(2,1)} %all-gather.2.cloned.1.call-done) | data formatting | bytes 16777216 | tf_op jit(solution)/shard_map/all_gather | solution.py:22
  192.1 9.4 %fusion.4 = bf16[8,64,1,4096]{3,1,0,2:T(8,128)(2,1)} fusion(bf16[2,512,1,4096]{3,1,0,2:T(8,128)(2,1)} %copy.8, bf16[8,64,2,512]{3,2,1,0:T(2,128)(2,1)S(1)} %multiply_multiply_fusion), kind=kOutput, calls=%fused_computation.3 | convolution fusion | flops 4297064448 | bytes 13631488 | tf_op jit(solution)/shard_map/iakc,kcjb->iajb/dot_general | solution.py:19
  201.5 10.0 %copy.10 = bf16[8,64,1,4096]{1,0,2,3:T(8,128)(2,1)} copy(bf16[8,64,1,4096]{3,1,0,2:T(8,128)(2,1)} %fusion.4) | data formatting | bytes 8388608 | tf_op jit(solution)/shard_map/convert_element_type | solution.py:26
  211.5 14.3 %reshape.15 = bf16[64,2,16384]{2,1,0:T(2,128)(2,1)} reshape(bf16[4096,1,8,64]{3,2,1,0:T(8,128)(2,1)} %bitcast.25) | data formatting | bytes 8388608
  225.8 187.9 %all_to_all.18 = bf16[64,2,16384]{2,1,0:T(2,128)(2,1)} all-to-all(bf16[64,2,16384]{2,1,0:T(2,128)(2,1)} %reshape.15), channel_id=1, replica_groups=mesh['tr'=64,'ct'=8] {'tr'}, dimensions={0} | all-to-all | bytes 8388608 | tf_op jit(solution)/shard_map/all_to_all | solution.py:25
  413.8 14.6 %reshape.16 = bf16[4096,1,8,64]{3,2,1,0:T(8,128)(2,1)} reshape(bf16[64,2,16384]{2,1,0:T(2,128)(2,1)} %all_to_all.18) | data formatting | bytes 8388608
  428.4 12.0 %copy.11 = bf16[8,64,64,1,64]{2,1,4,0,3:T(8,128)(2,1)} copy(bf16[8,64,64,1,64]{2,0,4,1,3:T(8,128)(2,1)} %bitcast.26) | data formatting | bytes 8388608 | tf_op jit(solution)/shard_map/all_to_all | solution.py:25
  440.4 12.1 %all_to_all.16 = bf16[8,4096,1,64]{1,3,2,0:T(8,128)(2,1)} reshape(bf16[8,64,64,1,64]{2,1,4,0,3:T(8,128)(2,1)} %copy.11) | data formatting | bytes 8388608 | tf_op jit(solution)/shard_map/all_to_all | solution.py:25
  452.4 0.0 reduce-scatter.2.cloned.1.call-update
  452.4 41.4 %reduce-scatter.2.cloned.1.call-done = bf16[1,4096,1,64]{1,3,2,0:T(8,128)(2,1)} async-done(((bf16[8,4096,1,64]{1,3,2,0:T(8,128)(2,1)}), bf16[1,4096,1,64]{1,3,2,0:T(8,128)(2,1)}) %reduce-scatter.2.cloned.1.call-update) | async-done | bytes 524304 | tf_op jit(solution)/shard_map/reduce_scatter | solution.py:28
  (1 shorter events, 0.0 us)
Async XLA Ops:
  6.5 164.3 %all-gather.2.cloned.1.call-start = ((), (), s32[]{:S(2)}) async-start(), calls=%async_computation.2 | async-start | bytes 8519680 | tf_op jit(solution)/shard_map/all_gather | solution.py:22
  8.3 485.6 %reduce-scatter.2.cloned.1.call-start = ((), (), s32[]{:S(2)}) async-start(), calls=%async_computation.3 | async-start | bytes 4718592 | tf_op jit(solution)/shard_map/reduce_scatter | solution.py:28
Sparse Core Ops, SparseCore 0:
  10.3 160.4 all-gather.1
  452.6 41.2 reduce-scatter.1
where the time goes:
time: 503 us; the launch traced here: 501 us
  waiting for transfers between devices  200 us (40%)
  blocking collectives  188 us (37%)
  local copies, waits for them, and re-layouts  86.8 us (17%)
  between operations  13.4 us (3%)
  matrix products  9.39 us (2%)
    all_to_all x1, blocking collectives, per_device(): lax.all_to_all(partial_value.astype(jnp.bfloat16), 'tr', split_axis=3, co...  188 us
    all_gather x1, waiting for transfers between devices, per_device(): lax.all_gather(cycle_integrals, 'tr', axis=3, tiled=True)  158 us
    reduce_scatter x1, waiting for transfers between devices, per_device(): lax.psum_scatter(moved_parts.astype(jnp.float32).astype(jnp.bfloat16), 'c...  41.4 us
    unnamed x3, local copies, waits for them, and re-layouts  30.6 us
    all_to_all x2, local copies, waits for them, and re-layouts, per_device(): lax.all_to_all(partial_value.astype(jnp.bfloat16), 'tr', split_axis=3, co...  24 us
    all_gather x1, local copies, waits for them, and re-layouts, per_device(): lax.all_gather(cycle_integrals, 'tr', axis=3, tiled=True)  21.3 us
  transfers between devices with their start and end apart: 2, of which 2 were waited for; matrix products, arithmetic and copies ran while one was open for 1% of the time, Pallas kernels for 0%

commit v1 on v0

--- a/solution.py
+++ b/solution.py
@@ -1,7 +1,23 @@
+import functools
 import jax
 import jax.numpy as jnp
 from jax import lax
 from jax.sharding import PartitionSpec as P
+
+
+def define_domain_over_axis(z, along_axis):
+    return jnp.concatenate(
+        lax.all_to_all(
+            jnp.stack([z] * lax.axis_size(along_axis), axis=0),
+            axis_name=along_axis,
+            split_axis=0,
+            concat_axis=0,
+        ),
+        axis=3,
+    )
+
+
+drive_the_meshes = functools.partial(define_domain_over_axis, along_axis="tr")
 
 
 def per_device(amplitudes, cycle_integrals, pair_live):
@@ -19,7 +35,7 @@
     partial_value = jnp.einsum(
         "iakc,kcjb->iajb",
         masked,
-        lax.all_gather(cycle_integrals, "tr", axis=3, tiled=True),
+        drive_the_meshes(cycle_integrals),
         preferred_element_type=jnp.float32,
     )
     moved_parts = lax.all_to_all(

time: 503 us -> 721 us (1.43)
  the two profiles are of different devices: /device:TPU:2 before, /device:TPU:6 now
where the time goes in v1:
time: 721 us; the launch traced here: 719 us
  waiting for transfers between devices  403 us (56%)
  blocking collectives  197 us (27%)
  local copies, waits for them, and re-layouts  76.1 us (11%)
  starting transfers between devices  19.2 us (3%)
  between operations  13.5 us (2%)
  matrix products  9.52 us (1%)
    all_to_all x1, waiting for transfers between devices, define_domain_over_axis(): lax.all_to_all(jnp.stack([z] * lax.axis_size(along_axis), axis=0), axis_n...  364 us
    all_to_all x1, blocking collectives, per_device(): lax.all_to_all(partial_value.astype(jnp.bfloat16), 'tr', split_axis=3, co...  197 us
    reduce_scatter x1, waiting for transfers between devices, per_device(): lax.psum_scatter(moved_parts.astype(jnp.float32).astype(jnp.bfloat16), 'c...  38.8 us
    unnamed x6, local copies, waits for them, and re-layouts  28.9 us
    all_to_all x2, local copies, waits for them, and re-layouts, per_device(): lax.all_to_all(partial_value.astype(jnp.bfloat16), 'tr', split_axis=3, co...  24 us
    all_to_all x1, starting transfers between devices, define_domain_over_axis(): lax.all_to_all(jnp.stack([z] * lax.axis_size(along_axis), axis=0), axis_n...  19.1 us
  transfers between devices with their start and end apart: 2, of which 2 were waited for; matrix products, arithmetic and copies ran while one was open for 0% of the time, Pallas kernels for 0%

profile of v1, /device:TPU:6, one launch (start us, length us, event | category | flops | bytes accessed | tf_op | source)
XLA Modules:
  0.0 719.5 jit_solution(9117766954884938592)
XLA Ops:
  6.5 5.2 stack.2
  11.7 0.0 copy-start.1
  11.7 0.0 slice-start
  11.7 0.0 copy-start
  11.7 19.1 %all-to-all-start = ((bf16[64,2,512,1,64]{2,4,1,3,0:T(8,128)(2,1)}), bf16[64,2,512,1,64]{2,4,1,3,0:T(8,128)(2,1)}, u32[]{:S(2)}, u32[]{:S(2)}) async-start(bf16[64,2,512,1,64]{2,4,1,3,0:T(8,128)(2,1)} %stack.2), calls=%async_computation | async-start | bytes 16777216 | tf_op jit(solution)/shard_map/all_to_all | solution.py:10
  30.8 0.0 reduce-scatter.2.cloned.1.call-start
  30.9 0.0 copy-done.1
  30.9 0.2 fusion.2
  31.1 0.0 slice-done
  31.1 0.1 broadcast_in_dim.2
  31.2 0.1 reshape.18
  31.3 0.0 copy-done
  31.3 1.1 multiply_multiply_fusion
  32.4 363.9 %all-to-all-done = bf16[64,2,512,1,64]{2,4,1,3,0:T(8,128)(2,1)} async-done(((bf16[64,2,512,1,64]{2,4,1,3,0:T(8,128)(2,1)}), bf16[64,2,512,1,64]{2,4,1,3,0:T(8,128)(2,1)}, u32[]{:S(2)}, u32[]{:S(2)}) %all-to-all-start) | async-done | bytes 8388640 | tf_op jit(solution)/shard_map/all_to_all | solution.py:10
  396.3 7.7 %copy.10 = bf16[64,2,512,1,64]{2,4,0,1,3:T(8,128)(2,1)} copy(bf16[64,2,512,1,64]{2,4,1,3,0:T(8,128)(2,1)} %all-to-all-done) | data formatting | bytes 16777216 | tf_op jit(solution)/shard_map/all_to_all | solution.py:10
  404.0 9.5 %fusion = bf16[8,64,1,4096]{3,1,0,2:T(8,128)(2,1)} fusion(bf16[2,512,4096,1]{1,2,0,3:T(8,128)(2,1)} %bitcast.26, bf16[8,64,2,512]{3,2,1,0:T(2,128)(2,1)S(1)} %multiply_multiply_fusion), kind=kOutput, calls=%fused_computation.1 | convolution fusion | flops 4297064448 | bytes 13631488 | tf_op jit(solution)/shard_map/iakc,kcjb->iajb/dot_general | solution.py:35
  413.5 10.0 %copy.13 = bf16[8,64,1,4096]{1,0,2,3:T(8,128)(2,1)} copy(bf16[8,64,1,4096]{3,1,0,2:T(8,128)(2,1)} %fusion) | data formatting | bytes 8388608 | tf_op jit(solution)/shard_map/convert_element_type | solution.py:42
  423.6 14.3 %reshape.24 = bf16[64,2,16384]{2,1,0:T(2,128)(2,1)} reshape(bf16[4096,1,8,64]{3,2,1,0:T(8,128)(2,1)} %bitcast.24) | data formatting | bytes 8388608
  437.9 197.3 %all_to_all.23 = bf16[64,2,16384]{2,1,0:T(2,128)(2,1)} all-to-all(bf16[64,2,16384]{2,1,0:T(2,128)(2,1)} %reshape.24), channel_id=1, replica_groups=mesh['tr'=64,'ct'=8] {'tr'}, dimensions={0} | all-to-all | bytes 8388608 | tf_op jit(solution)/shard_map/all_to_all | solution.py:41
  635.1 14.6 %reshape.25 = bf16[4096,1,8,64]{3,2,1,0:T(8,128)(2,1)} reshape(bf16[64,2,16384]{2,1,0:T(2,128)(2,1)} %all_to_all.23) | data formatting | bytes 8388608
  649.7 12.0 %copy.14 = bf16[8,64,64,1,64]{2,1,4,0,3:T(8,128)(2,1)} copy(bf16[8,64,64,1,64]{2,0,4,1,3:T(8,128)(2,1)} %bitcast.25) | data formatting | bytes 8388608 | tf_op jit(solution)/shard_map/all_to_all | solution.py:41
  661.7 12.0 %all_to_all.20 = bf16[8,4096,1,64]{1,3,2,0:T(8,128)(2,1)} reshape(bf16[8,64,64,1,64]{2,1,4,0,3:T(8,128)(2,1)} %copy.14) | data formatting | bytes 8388608 | tf_op jit(solution)/shard_map/all_to_all | solution.py:41
  673.8 0.0 reduce-scatter.2.cloned.1.call-update
  673.8 38.8 %reduce-scatter.2.cloned.1.call-done = bf16[1,4096,1,64]{1,3,2,0:T(8,128)(2,1)} async-done(((bf16[8,4096,1,64]{1,3,2,0:T(8,128)(2,1)}), bf16[1,4096,1,64]{1,3,2,0:T(8,128)(2,1)}) %reduce-scatter.2.cloned.1.call-update) | async-done | bytes 524304 | tf_op jit(solution)/shard_map/reduce_scatter | solution.py:44
  (1 shorter events, 0.0 us)
Async XLA Ops:
  11.7 19.2 %copy-start.1 = (s32[8,64]{1,0:T(8,128)S(1)}, s32[8,64]{1,0:T(8,128)}, u32[]{:S(2)}) copy-start(s32[8,64]{1,0:T(8,128)} %param.5) | copy-start | bytes 6148
  11.7 19.4 %slice-start = ((s32[8,64]{1,0:T(8,128)}), s32[2,64]{1,0:T(2,128)S(1)}, s32[]{:S(2)}) async-start(s32[8,64]{1,0:T(8,128)} %param.5), calls=%async_computation.4 | async-start | bytes 2048 | tf_op jit(solution)/shard_map/slice | solution.py:30
  11.7 19.6 %copy-start = (bf16[8,64,2,512]{3,2,1,0:T(2,128)(2,1)S(1)}, bf16[8,64,2,512]{3,2,1,0:T(2,128)(2,1)}, u32[]{:S(2)}) copy-start(bf16[8,64,2,512]{3,2,1,0:T(2,128)(2,1)} %param.3) | copy-start | bytes 3145732
  11.7 384.6 %all-to-all-start = ((bf16[64,2,512,1,64]{2,4,1,3,0:T(8,128)(2,1)}), bf16[64,2,512,1,64]{2,4,1,3,0:T(8,128)(2,1)}, u32[]{:S(2)}, u32[]{:S(2)}) async-start(bf16[64,2,512,1,64]{2,4,1,3,0:T(8,128)(2,1)} %stack.2), calls=%async_computation | async-start | bytes 16777216 | tf_op jit(solution)/shard_map/all_to_all | solution.py:10
  30.8 681.8 %reduce-scatter.2.cloned.1.call-start = ((), (), s32[]{:S(2)}) async-start(), calls=%async_computation.3 | async-start | bytes 4718592 | tf_op jit(solution)/shard_map/reduce_scatter | solution.py:44
Sparse Core Ops, SparseCore 0:
  673.9 38.6 reduce-scatter.1

commit v2 on v0

--- a/solution.py
+++ b/solution.py
@@ -22,9 +22,12 @@
         lax.all_gather(cycle_integrals, "tr", axis=3, tiled=True),
         preferred_element_type=jnp.float32,
     )
-    moved_parts = lax.all_to_all(
-        partial_value.astype(jnp.bfloat16), "tr", split_axis=3, concat_axis=1, tiled=True
-    )
+    piece_in = partial_value.astype(jnp.bfloat16)
+    side_arr = lax.axis_size("tr")
+    shaped = jnp.split(piece_in, side_arr, axis=3)
+    high = jnp.stack(shaped)
+    inter = lax.all_to_all(high, "tr", 0, 0)
+    moved_parts = jnp.concatenate(inter, axis=1)
     moved = lax.psum_scatter(
         moved_parts.astype(jnp.float32).astype(jnp.bfloat16), "ct", scatter_dimension=0, tiled=True
     )

time: 503 us -> 511 us (1.016)
  local copies, waits for them, and re-layouts: 86.8 us -> 96.1 us
    reshape x0 -> x3, local copies, waits for them, and re-layouts: none -> 34.5 us  [per_device(): moved_parts = jnp.concatenate(inter, axis=1)]
    all_to_all x2 -> x0, local copies, waits for them, and re-layouts: 24 us -> none  [per_device(): lax.all_to_all(partial_value.astype(jnp.bfloat16), 'tr', split_axis=3, co...]
    convert_element_type x1 -> x0, local copies, waits for them, and re-layouts: 10 us -> none  [per_device(): partial_value.astype(jnp.bfloat16)]
    unnamed x3 -> x68, local copies, waits for them, and re-layouts: 30.6 us -> 39.4 us
where the time goes in v2:
time: 511 us; the launch traced here: 509 us
  waiting for transfers between devices  200 us (39%)
  blocking collectives  188 us (37%)
  local copies, waits for them, and re-layouts  96.1 us (19%)
  between operations  13.7 us (3%)
  matrix products  8.08 us (2%)
    all_to_all x1, blocking collectives, per_device(): inter = lax.all_to_all(high, 'tr', 0, 0)  188 us
    all_gather x1, waiting for transfers between devices, per_device(): lax.all_gather(cycle_integrals, 'tr', axis=3, tiled=True)  158 us
    reduce_scatter x1, waiting for transfers between devices, per_device(): lax.psum_scatter(moved_parts.astype(jnp.float32).astype(jnp.bfloat16), 'c...  41.4 us
    unnamed x68, local copies, waits for them, and re-layouts  39.4 us
    reshape x3, local copies, waits for them, and re-layouts, per_device(): moved_parts = jnp.concatenate(inter, axis=1)  34.5 us
    all_gather x1, local copies, waits for them, and re-layouts, per_device(): lax.all_gather(cycle_integrals, 'tr', axis=3, tiled=True)  21.2 us
  transfers between devices with their start and end apart: 2, of which 2 were waited for; matrix products, arithmetic and copies ran while one was open for 1% of the time, Pallas kernels for 0%

profile of v2, /device:TPU:2, one launch (start us, length us, event | category | flops | bytes accessed | tf_op | source)
XLA Modules:
  0.0 508.9 jit_solution(9158225113865171625)
XLA Ops:
  6.5 1.7 copy.10
  8.3 0.7 slice.3
  9.0 0.9 fusion.8
  10.1 2.3 multiply_multiply_fusion
  12.4 158.5 %all-gather.2.cloned.1.call-done = bf16[2,512,1,4096]{1,0,2,3:T(2,128)(2,1)} async-done(((bf16[2,512,1,64]{1,0,2,3:T(2,128)(2,1)}), bf16[2,512,1,4096]{1,0,2,3:T(2,128)(2,1)}) %all-gather.2.cloned.1.call-update) | async-done | bytes 8388624 | tf_op jit(solution)/shard_map/all_gather | solution.py:22
  170.8 21.2 %copy.11 = bf16[2,512,1,4096]{3,1,0,2:T(8,128)(2,1)} copy(bf16[2,512,1,4096]{1,0,2,3:T(2,128)(2,1)} %all-gather.2.cloned.1.call-done) | data formatting | bytes 16777216 | tf_op jit(solution)/shard_map/all_gather | solution.py:22
  192.0 8.1 %fusion.4 = bf16[8,64,1,4096]{3,1,0,2:T(8,128)(2,1)S(1)} fusion(bf16[2,512,1,4096]{3,1,0,2:T(8,128)(2,1)} %copy.11, bf16[8,64,2,512]{3,2,1,0:T(2,128)(2,1)S(1)} %multiply_multiply_fusion), kind=kOutput, calls=%fused_computation.3 | convolution fusion | flops 4297064448 | bytes 13631488 | tf_op jit(solution)/shard_map/iakc,kcjb->iajb/dot_general | solution.py:19
  200.5 0.1 constant_dynamic-update-slice_fusion.58
  200.9 0.1 constant_dynamic-update-slice_fusion.54
  201.1 0.1 constant_dynamic-update-slice_fusion.52
  202.2 0.1 constant_dynamic-update-slice_fusion.40
  202.4 0.1 constant_dynamic-update-slice_fusion.38
  202.8 0.1 constant_dynamic-update-slice_fusion.34
  203.2 0.1 constant_dynamic-update-slice_fusion.30
  203.3 0.1 constant_dynamic-update-slice_fusion.28
  203.5 0.1 constant_dynamic-update-slice_fusion.26
  206.1 3.2 copy-done
  209.3 14.3 %reshape.23 = bf16[64,2,16384]{2,1,0:T(2,128)(2,1)} reshape(bf16[64,1,8,64,64]{4,3,2,1,0:T(8,128)(2,1)} %bitcast.283) | data formatting | bytes 8388608
  223.6 187.9 %all_to_all.5 = bf16[64,2,16384]{2,1,0:T(2,128)(2,1)} all-to-all(bf16[64,2,16384]{2,1,0:T(2,128)(2,1)} %reshape.23), channel_id=1, replica_groups=mesh['tr'=64,'ct'=8] {'tr'}, dimensions={0} | all-to-all | bytes 8388608 | tf_op jit(solution)/shard_map/all_to_all | solution.py:29
  411.6 14.6 %reshape.24 = bf16[64,1,8,64,64]{4,3,2,1,0:T(8,128)(2,1)} reshape(bf16[64,2,16384]{2,1,0:T(2,128)(2,1)} %all_to_all.5) | data formatting | bytes 8388608
  426.2 10.3 %bitcast_bitcast_fusion = bf16[8,64,64,1,64]{4,2,0,3,1:T(8,128)(2,1)} fusion(bf16[64,1,8,64,64]{4,3,2,1,0:T(8,128)(2,1)} %reshape.24), kind=kLoop, calls=%fused_computation.137 | loop fusion | bytes 8388608 | tf_op jit(solution)/shard_map/reshape | solution.py:30
  436.5 12.1 %copy.13 = bf16[8,64,64,1,64]{2,1,4,0,3:T(8,128)(2,1)} copy(bf16[8,64,64,1,64]{4,2,0,3,1:T(8,128)(2,1)} %bitcast_bitcast_fusion) | data formatting | bytes 8388608 | tf_op jit(solution)/shard_map/reshape | solution.py:30
  448.6 12.0 %reshape.19 = bf16[8,4096,1,64]{1,3,0,2:T(8,128)(2,1)} reshape(bf16[8,64,64,1,64]{2,1,4,0,3:T(8,128)(2,1)} %copy.13) | data formatting | bytes 8388608 | tf_op jit(solution)/shard_map/reshape | solution.py:30
  460.7 41.4 %reduce-scatter.2.cloned.1.call-done = bf16[1,4096,1,64]{1,3,0,2:T(8,128)(2,1)} async-done(((bf16[8,4096,1,64]{1,3,0,2:T(8,128)(2,1)}), bf16[1,4096,1,64]{1,3,0,2:T(8,128)(2,1)}) %reduce-scatter.2.cloned.1.call-update) | async-done | bytes 524304 | tf_op jit(solution)/shard_map/reduce_scatter | solution.py:31
  (63 shorter events, 4.9 us)
Async XLA Ops:
  6.5 164.3 %all-gather.2.cloned.1.call-start = ((), (), s32[]{:S(2)}) async-start(), calls=%async_computation.2 | async-start | bytes 8519680 | tf_op jit(solution)/shard_map/all_gather | solution.py:22
  8.3 493.8 %reduce-scatter.2.cloned.1.call-start = ((), (), s32[]{:S(2)}) async-start(), calls=%async_computation.3 | async-start | bytes 4718592 | tf_op jit(solution)/shard_map/reduce_scatter | solution.py:31
  206.1 3.2 copy-start
Sparse Core Ops, SparseCore 0:
  10.3 160.4 all-gather.1
  460.8 41.2 reduce-scatter.1
